TPU v7x, 256 devices: a whole 4x4x8 slice. The times are simulated.
256 devices in a mesh: date: 16 (over z, core), tile: 16 (over x, y).
Axes of the slice: x: 4, y: 4, z: 8, core: 2. Of those that a mesh axis runs over, the one named last changes fastest.
Arguments:
- imagery: bfloat16 [10, 64, 65536], P(None, 'date', 'tile'), may hold values from -6 to 6
- owner: int32 [65536, 1], replicated, may hold values from 0 to 15; in each aligned block of 4096 rows (0 to 4095, 4096 to 8191, ...) at most 1024 rows name the same one
- parcel_local: int32 [65536], replicated, may hold values from 0 to 15
- lift_weight: bfloat16 [10, 128], replicated, may hold values from -2 to 2
- depth_weight: float32 [2, 5, 128], replicated, may hold values from -2.5 to 2.5
- point_weight: bfloat16 [2, 128, 128], replicated, may hold values from -0.5 to 0.5
- bn_mean: float32 [2, 128], replicated, may hold values from -0.5 to 0.5
- bn_var: float32 [2, 128], replicated, may hold values from 0.25 to 4
- bn_gain: float32 [2, 128], replicated, may hold values from 0.5 to 2
- bn_shift: float32 [2, 128], replicated, may hold values from -1 to 1
Outputs:
- parcel_means: float32 [16, 256, 128], P('date', 'tile')
Inputs may be any that keep to these rules, and one draw needn't show every extreme that they name: `owner`: in each aligned block of 4096 rows (the pixels of one tile), no tile index appears more than 1024 times, and some index appears exactly 1024 times.
All inputs are finite; a program needn't handle non-finite values.
Results may differ from a plain program's by a relative error of at most 0.0008.
Values may be sent and summed in bfloat16 or wider, within the bound.
No kernel may reach another device: no remote copies, remote signals or barrier semaphores. Data moves between devices by JAX's collectives and lax.ppermute only.
A program may use at most 128 MiB of HBM per device.

v0:
```python
import math
import jax
import jax.numpy as jnp
from jax import lax
from jax.sharding import PartitionSpec as P

PARC_DEV = 16
epsilon = 1e-05


def layer_stack(series, weights):
    lift_weight, depth_weight, point_weight, bn_mean, bn_var, bn_gain, bn_shift = weights
    hidden = jnp.einsum(
        "bts,bc->tsc", series, lift_weight, preferred_element_type=jnp.float32
    ).astype(jnp.bfloat16)
    for layer in range(depth_weight.shape[0]):
        length = hidden.shape[0]
        half = depth_weight.shape[1] // 2
        widened = jnp.pad(hidden, ((half, half), (0, 0), (0, 0)))
        spread = jnp.zeros(hidden.shape, jnp.float32)
        for tap in range(depth_weight.shape[1]):
            spread = spread + depth_weight[layer, tap] * widened[tap : tap + length]
        spread = spread.astype(jnp.bfloat16)
        mixed = jnp.einsum(
            "tsc,cd->tsd", spread, point_weight[layer], preferred_element_type=jnp.float32
        )
        factor = bn_gain[layer] / jnp.sqrt(bn_var[layer] + epsilon)
        normed = jax.nn.relu((mixed - bn_mean[layer]) * factor + bn_shift[layer])
        hidden = (0.5 * (normed[0::2] + normed[1::2])).astype(jnp.bfloat16)
    return hidden


def local(
    imagery,
    owner,
    parcel_local,
    lift_weight,
    depth_weight,
    point_weight,
    bn_mean,
    bn_var,
    bn_gain,
    bn_shift,
):
    weights = (lift_weight, depth_weight, point_weight, bn_mean, bn_var, bn_gain, bn_shift)
    tiles = lax.axis_size("tile")
    dates = lax.axis_size("date")
    tile_index = lax.axis_index("tile")
    date_index = lax.axis_index("date")
    bands, date_dev, pix_dev = imagery.shape
    owners = owner[:, 0]
    mine = owners == tile_index
    catalog = jnp.arange(PARC_DEV, dtype=jnp.int32)
    counts = jnp.sum(
        ((parcel_local[:, None] == catalog[None, :]) & mine[:, None]).astype(jnp.int32), axis=0
    )
    capacity = 4 * pix_dev // max(tiles, 8)
    share = capacity // dates
    owner_ids = jnp.arange(tiles, dtype=jnp.int32)
    positions = jnp.arange(pix_dev, dtype=jnp.int32)
    own_owner = lax.dynamic_slice_in_dim(owners, tile_index * pix_dev, pix_dev, 0)
    onehot = (own_owner[:, None] == owner_ids[None, :]).astype(jnp.int32)
    running = jnp.cumsum(onehot, axis=0)
    own_rank = jnp.sum(running * onehot, axis=1) - 1
    own_count = jnp.sum(onehot, axis=0)
    table = (
        jnp.zeros((tiles * capacity,), jnp.int32).at[own_owner * capacity + own_rank].set(positions)
    )
    table = table.reshape(tiles, share, dates).transpose(2, 0, 1).reshape(-1)
    rank_send = (
        jnp.arange(share, dtype=jnp.int32)[None, None, :] * dates
        + jnp.arange(dates, dtype=jnp.int32)[:, None, None]
    )
    valid_send = (rank_send < own_count[None, :, None]).reshape(-1)
    rows = imagery.reshape(bands * date_dev, pix_dev).T
    picked = jnp.take(rows, table, axis=0)
    picked = jnp.where(valid_send[:, None], picked, jnp.zeros_like(picked))
    outgoing = picked.T.reshape(bands, date_dev, table.shape[0])
    arrived = lax.all_to_all(
        lax.all_to_all(outgoing, "date", split_axis=2, concat_axis=1, tiled=True),
        "tile",
        split_axis=2,
        concat_axis=2,
        tiled=True,
    )
    grid = owners.reshape(tiles, pix_dev)
    mine_grid = (grid == tile_index).astype(jnp.int32)
    recv_rank = jnp.cumsum(mine_grid, axis=1) - 1
    target = jnp.where(mine_grid == 1, owner_ids[:, None] * capacity + recv_rank, tiles * capacity)
    recv_table = (
        jnp.full((tiles * capacity + 1,), -1, jnp.int32).at[target.reshape(-1)].set(parcel_local)
    )
    slot_ranks = jnp.arange(share, dtype=jnp.int32) * dates + date_index
    slot_parcel = jnp.take(recv_table[:-1].reshape(tiles, capacity), slot_ranks, axis=1).reshape(-1)
    slots = arrived.shape[2]
    block = math.gcd(slots, 512)
    nblocks = slots // block
    pieces = arrived.reshape(bands, arrived.shape[1], nblocks, block).transpose(2, 0, 1, 3)
    labels = slot_parcel.reshape(nblocks, block)

    def run_block(item):
        piece, label = item
        features = layer_stack(piece, weights)
        member = (label[None, :] == catalog[:, None]).astype(jnp.bfloat16)
        return jnp.einsum("qs,jsc->jqc", member, features, preferred_element_type=jnp.float32)

    partial_value = jnp.sum(lax.map(run_block, (pieces, labels)), axis=0)
    sums = lax.psum_scatter(partial_value, "date", scatter_dimension=0, tiled=True)
    return sums / jnp.maximum(counts, 1).astype(jnp.float32)[None, :, None]


def solution(mesh):
    placed = (P(None, "date", "tile"), P(), P(), P(), P(), P(), P(), P(), P(), P())
    return jax.shard_map(
        local, mesh=mesh, in_specs=placed, out_specs=P("date", "tile", None), check_vma=False
    )
```

profile of v0, /device:TPU:4, one launch (start us, length us, event | category | flops | bytes accessed | tf_op | source)
XLA Modules:
  0.0 670.8 jit_solution(5873517295143704459)
XLA Ops:
  7.3 4.6 reduce-window.14
  13.7 15.6 %scatter_custom_fusion = s32[16384]{0:T(1024)S(1)} fusion(s32[4096]{0:T(1024)S(1)} %bitcast.142, s32[4096]{0:T(1024)S(1)} %iota.39, s32[]{:T(128)} %copy.70), kind=kCustom, calls=%fused_computation.86 | custom fusion | bytes 65540 | tf_op jit(solution)/shard_map/scatter | solution.py:67
  30.1 1.1 reshape.262
  31.8 57.4 %gather_fusion = bf16[16384,40]{1,0:T(8,128)(2,1)} fusion(bf16[4096,40]{1,0:T(8,128)(2,1)S(1)} %bitcast.121, s32[16384]{0:T(1024)S(1)} %broadcast_clamp_fusion), kind=kCustom, calls=%fused_computation | custom fusion | bytes 2686976 | tf_op jit(solution)/shard_map/jit(_take)/gather | solution.py:76
  89.2 13.9 %select_bitcast_fusion = bf16[40,16384]{0,1:T(8,128)(2,1)} fusion(bf16[16384,40]{1,0:T(8,128)(2,1)} %gather_fusion, pred[16384]{0:T(1024)(128)(4,1)S(1)} %compare_and_fusion, pred[16384]{0:T(1024)(128)(4,1)S(1)} %lt.84), kind=kLoop, calls=%fused_computation.60 | loop fusion | flops 1310720 | bytes 2654208 | tf_op jit(solution)/shard_map/jit(_where)/select_n | solution.py:77
  103.1 3.5 copy.49
  107.1 16.3 %copy.50 = bf16[10,4,16384]{0,1,2:T(4,128)(2,1)} copy(bf16[10,4,16384]{2,1,0:T(4,128)(2,1)S(1)} %reshape.264) | data formatting | bytes 2621440 | tf_op jit(solution)/shard_map/reshape | solution.py:78
  123.4 27.2 %reshape.312 = bf16[16,2,20480]{2,1,0:T(2,128)(2,1)} reshape(bf16[16384,4,10]{2,1,0:T(4,128)(2,1)} %bitcast.122) | data formatting | bytes 2621440
  150.6 8.6 %all-to-all-start = ((bf16[16,2,20480]{2,1,0:T(2,128)(2,1)}), bf16[16,2,20480]{2,1,0:T(2,128)(2,1)S(1)}, u32[]{:S(2)}, u32[]{:S(2)}) async-start(bf16[16,2,20480]{2,1,0:T(2,128)(2,1)} %reshape.312), calls=%async_computation | async-start | bytes 2621440 | tf_op jit(solution)/shard_map/all_to_all | solution.py:80
  159.6 1.4 compare_reduce_fusion
  161.0 4.6 reduce-window.16
  166.4 24.9 %all-to-all-done = bf16[16,2,20480]{2,1,0:T(2,128)(2,1)S(1)} async-done(((bf16[16,2,20480]{2,1,0:T(2,128)(2,1)}), bf16[16,2,20480]{2,1,0:T(2,128)(2,1)S(1)}, u32[]{:S(2)}, u32[]{:S(2)}) %all-to-all-start) | async-done | bytes 1310752 | tf_op jit(solution)/shard_map/all_to_all | solution.py:80
  191.4 40.8 %reshape.313 = bf16[16384,4,10]{2,1,0:T(4,128)(2,1)} reshape(bf16[16,2,20480]{2,1,0:T(2,128)(2,1)S(1)} %all-to-all-done) | data formatting | bytes 2621440
  232.2 23.6 %copy.51 = bf16[10,4,16,1024]{3,1,2,0:T(4,128)(2,1)S(1)} copy(bf16[10,4,16,1024]{0,1,3,2:T(4,128)(2,1)} %bitcast.123) | data formatting | bytes 2621440 | tf_op jit(solution)/shard_map/all_to_all | solution.py:80
  256.1 4.8 copy.52
  260.9 6.5 reshape.314
  267.5 7.5 %all-to-all-start.1 = ((bf16[16,2,20480]{2,1,0:T(2,128)(2,1)}), bf16[16,2,20480]{2,1,0:T(2,128)(2,1)S(1)}, u32[]{:S(2)}, u32[]{:S(2)}) async-start(bf16[16,2,20480]{2,1,0:T(2,128)(2,1)} %reshape.314), calls=%async_computation.1 | async-start | bytes 2621440 | tf_op jit(solution)/shard_map/all_to_all | solution.py:79
  275.7 240.0 %scatter_custom_fusion.1 = s32[16385]{0:T(1024)S(1)} fusion(s32[65536]{0:T(1024)S(1)} %bitcast.134, s32[65536]{0:T(1024)} %param.14, s32[]{:T(128)} %constant.109.clone.1), kind=kCustom, calls=%fused_computation.83 | custom fusion | bytes 66052 | tf_op jit(solution)/shard_map/scatter | solution.py:91
  516.8 3.6 reshape.315
  520.5 7.4 %copy.58 = bf16[10,64,2,512]{3,2,1,0:T(2,128)(2,1)S(1)} copy(bf16[10,64,2,512]{1,0,3,2:T(8,128)(2,1)} %bitcast.125) | data formatting | bytes 2621440 | tf_op jit(solution)/shard_map/reshape | solution.py:98
  528.7 77.0 %while.13 = (s32[]{:T(128)}, f32[2,16,16,128]{3,2,1,0:T(8,128)}, f32[2,5,128]{2,1,0:T(8,128)S(1)}, bf16[2,10,64,512]{3,1,2,0:T(8,128)(2,1)S(1)}, bf16[10,128]{1,...) while((s32[]{:T(128)}, f32[2,16,16,128]{3,2,1,0:T(8,128)}, ...), condition=%wide.region_9.10_spmd.clone, body=%wide.region_8.9_spmd.clone.sunk | while | flops 1861231104 | bytes 78875824 | solution.py:107
  529.0 4.7 convolution_convert_fusion.2
  533.7 21.0 %add_maximum_fusion.4 = f32[64,512,128]{2,1,0:T(8,128)} fusion(f32[128]{0:T(128)S(1)} %get-tuple-element.364, f32[128]{0:T(128)S(1)} %get-tuple-element.365, f32[128]{0:T(128)S(1)} %get-tuple-element.366, bf16[64,512,128]{2,1,0:T(8,128)(2,1)} %convolution_convert_fusion.2, f32[128]{0:T(128)S(1)} %get-tuple-element.367, ...), kind=kOutput, calls=%fused_computation.5.clone.1 | convolution fusion | flops 1153433600 | bytes 25202688 | tf_op jit(solution)/shard_map/while/body/eval_jaxpr/tsc,cd->tsd/dot_general | solution.py:24
  554.8 6.4 multiply_convert_fusion.10
  561.2 4.9 add_maximum_fusion.5
  567.4 4.7 convolution_convert_fusion.2
  572.1 21.0 %add_maximum_fusion.4 = f32[64,512,128]{2,1,0:T(8,128)} fusion(f32[128]{0:T(128)S(1)} %get-tuple-element.364, f32[128]{0:T(128)S(1)} %get-tuple-element.365, f32[128]{0:T(128)S(1)} %get-tuple-element.366, bf16[64,512,128]{2,1,0:T(8,128)(2,1)} %convolution_convert_fusion.2, f32[128]{0:T(128)S(1)} %get-tuple-element.367, ...), kind=kOutput, calls=%fused_computation.5.clone.1 | convolution fusion | flops 1153433600 | bytes 25202688 | tf_op jit(solution)/shard_map/while/body/eval_jaxpr/tsc,cd->tsd/dot_general | solution.py:24
  593.1 6.4 multiply_convert_fusion.10
  599.6 4.9 add_maximum_fusion.5
  605.7 1.6 reduce_sum.38
  608.1 54.4 %reduce-scatter.2.cloned.1.call-done = f32[1,16,128]{2,1,0:T(8,128)} async-done(((f32[16,16,128]{2,1,0:T(8,128)}), f32[1,16,128]{2,1,0:T(8,128)}) %reduce-scatter.2.cloned.1.call-update) | async-done | bytes 8208 | tf_op jit(solution)/shard_map/reduce_scatter | solution.py:108
  662.6 1.4 broadcast_divide_fusion
  (88 shorter events, 11.7 us)
Async XLA Ops:
  123.4 36.2 %copy-start = (s32[65536,1]{0,1:T(1,128)S(1)}, s32[65536,1]{0,1:T(1,128)}, u32[]{:S(2)}) copy-start(s32[65536,1]{0,1:T(1,128)} %param.13) | copy-start | bytes 786436
  150.6 40.8 %all-to-all-start = ((bf16[16,2,20480]{2,1,0:T(2,128)(2,1)}), bf16[16,2,20480]{2,1,0:T(2,128)(2,1)S(1)}, u32[]{:S(2)}, u32[]{:S(2)}) async-start(bf16[16,2,20480]{2,1,0:T(2,128)(2,1)} %reshape.312), calls=%async_computation | async-start | bytes 2621440 | tf_op jit(solution)/shard_map/all_to_all | solution.py:80
  255.8 20.0 %copy-start.10 = (f32[2,5,128]{2,0,1:T(2,128)S(1)}, f32[2,5,128]{2,0,1:T(2,128)}, u32[]{:S(2)}) copy-start(f32[2,5,128]{2,0,1:T(2,128)} %param.16) | copy-start | bytes 15364
  267.5 249.3 %all-to-all-start.1 = ((bf16[16,2,20480]{2,1,0:T(2,128)(2,1)}), bf16[16,2,20480]{2,1,0:T(2,128)(2,1)S(1)}, u32[]{:S(2)}, u32[]{:S(2)}) async-start(bf16[16,2,20480]{2,1,0:T(2,128)(2,1)} %reshape.314), calls=%async_computation.1 | async-start | bytes 2621440 | tf_op jit(solution)/shard_map/all_to_all | solution.py:79
  274.9 253.7 %copy-start.5 = (bf16[10,128]{1,0:T(8,128)(2,1)S(1)}, bf16[10,128]{1,0:T(8,128)(2,1)}, u32[]{:S(2)}) copy-start(bf16[10,128]{1,0:T(8,128)(2,1)} %param.15) | copy-start | bytes 7684
  274.9 253.7 %copy-start.6 = (f32[2,128]{1,0:T(2,128)S(1)}, f32[2,128]{1,0:T(2,128)}, u32[]{:S(2)}) copy-start(f32[2,128]{1,0:T(2,128)} %param.20) | copy-start | bytes 3076
  274.9 253.7 %copy-start.7 = (f32[2,128]{1,0:T(2,128)S(1)}, f32[2,128]{1,0:T(2,128)}, u32[]{:S(2)}) copy-start(f32[2,128]{1,0:T(2,128)} %param.19) | copy-start | bytes 3076
  275.0 253.7 %copy-start.8 = (f32[2,128]{1,0:T(2,128)S(1)}, f32[2,128]{1,0:T(2,128)}, u32[]{:S(2)}) copy-start(f32[2,128]{1,0:T(2,128)} %param.21) | copy-start | bytes 3076
  275.0 253.7 %copy-start.9 = (f32[2,128]{1,0:T(2,128)S(1)}, f32[2,128]{1,0:T(2,128)}, u32[]{:S(2)}) copy-start(f32[2,128]{1,0:T(2,128)} %param.18) | copy-start | bytes 3076
  275.0 253.7 %copy-start.11 = (bf16[2,128,128]{2,1,0:T(8,128)(2,1)S(1)}, bf16[2,128,128]{2,1,0:T(8,128)(2,1)}, u32[]{:S(2)}) copy-start(bf16[2,128,128]{2,1,0:T(8,128)(2,1)} %param.17) | copy-start | bytes 196612
  275.0 387.6 %reduce-scatter.2.cloned.1.call-start = ((), (), s32[]{:S(2)}) async-start(), calls=%async_computation.3 | async-start | bytes 139264 | tf_op jit(solution)/shard_map/reduce_scatter | solution.py:108
  528.7 78.7 %copy-start.1 = (s32[65536]{0:T(1024)S(1)}, s32[65536]{0:T(1024)}, u32[]{:S(2)}) copy-start(s32[65536]{0:T(1024)} %param.14) | copy-start | bytes 786436
  528.7 78.6 %copy-start.4 = (pred[65536]{0:T(1024)(128)(4,1)S(1)}, pred[65536]{0:T(1024)(128)(4,1)}, u32[]{:S(2)}) copy-start(pred[65536]{0:T(1024)(128)(4,1)} %get-tuple-element.276) | copy-start | bytes 196612
  561.2 5.0 copy-start.2
  566.6 0.7 copy-start.3
  599.6 5.0 copy-start.2
  605.0 0.7 copy-start.3
Sparse Core Ops, SparseCore 0:
  607.5 55.0 reduce-scatter.1
where the time goes:
time: 672 us; the launch traced here: 671 us
  local copies, waits for them, and re-layouts  455 us (68%)
  waiting for transfers between devices  79.4 us (12%)
  matrix products  62.3 us (9%)
  other arithmetic  43.7 us (7%)
  starting transfers between devices  16.1 us (2%)
  between operations  13.8 us (2%)
    scatter x1, local copies, waits for them, and re-layouts, local(): jnp.full((tiles * capacity + 1,), -1, jnp.int32).at[target.reshape(-1)]  240 us
    unnamed x28, local copies, waits for them, and re-layouts  79.4 us
    gather x1, local copies, waits for them, and re-layouts, local(): picked = jnp.take(rows, table, axis=0)  57.4 us
    reduce_scatter x1, waiting for transfers between devices, local(): lax.psum_scatter(partial_value, 'date', scatter_dimension=0, tiled=True)  54.4 us
    dot_general x4, matrix products, layer_stack(): jnp.einsum('tsc,cd->tsd', spread, point_weight[layer], preferred_element_...  52 us
    all_to_all x3, local copies, waits for them, and re-layouts, local(): lax.all_to_all(outgoing, 'date', split_axis=2, concat_axis=1, tiled=True)  28.7 us
    all_to_all x1, waiting for transfers between devices, local(): lax.all_to_all(outgoing, 'date', split_axis=2, concat_axis=1, tiled=True)  24.9 us
    reshape x2, local copies, waits for them, and re-layouts, local(): outgoing = picked.T.reshape(bands, date_dev, table.shape[0])  16.8 us
  transfers between devices with their start and end apart: 3, of which 2 were waited for; matrix products, arithmetic and copies ran while one was open for 37% of the time, Pallas kernels for 0%

commit v1 on v0

--- a/solution.py
+++ b/solution.py
@@ -76,12 +76,20 @@
     picked = jnp.take(rows, table, axis=0)
     picked = jnp.where(valid_send[:, None], picked, jnp.zeros_like(picked))
     outgoing = picked.T.reshape(bands, date_dev, table.shape[0])
-    arrived = lax.all_to_all(
-        lax.all_to_all(outgoing, "date", split_axis=2, concat_axis=1, tiled=True),
-        "tile",
-        split_axis=2,
-        concat_axis=2,
-        tiled=True,
+    arrived = jnp.concatenate(
+        lax.all_to_all(
+            jnp.stack(
+                jnp.split(
+                    lax.all_to_all(outgoing, "date", split_axis=2, concat_axis=1, tiled=True),
+                    lax.axis_size("tile"),
+                    axis=2,
+                )
+            ),
+            "tile",
+            0,
+            0,
+        ),
+        axis=2,
     )
     grid = owners.reshape(tiles, pix_dev)
     mine_grid = (grid == tile_index).astype(jnp.int32)

time: 672 us -> 679 us (1.010)
  local copies, waits for them, and re-layouts: 455 us -> 462 us
    unnamed x28 -> x43, local copies, waits for them, and re-layouts: 79.4 us -> 89.7 us
    all_to_all x3 -> x2, local copies, waits for them, and re-layouts: 28.7 us -> 23.9 us  [local(): lax.all_to_all(outgoing, 'date', split_axis=2, concat_axis=1, tiled=True)]
where the time goes in v1:
time: 679 us; the launch traced here: 678 us
  local copies, waits for them, and re-layouts  462 us (68%)
  waiting for transfers between devices  79.4 us (12%)
  matrix products  62.3 us (9%)
  other arithmetic  43.7 us (6%)
  starting transfers between devices  16.1 us (2%)
  between operations  13.8 us (2%)
    scatter x1, local copies, waits for them, and re-layouts, local(): jnp.full((tiles * capacity + 1,), -1, jnp.int32).at[target.reshape(-1)]  240 us
    unnamed x43, local copies, waits for them, and re-layouts  89.7 us
    gather x1, local copies, waits for them, and re-layouts, local(): picked = jnp.take(rows, table, axis=0)  57.4 us
    reduce_scatter x1, waiting for transfers between devices, local(): lax.psum_scatter(partial_value, 'date', scatter_dimension=0, tiled=True)  54.4 us
    dot_general x4, matrix products, layer_stack(): jnp.einsum('tsc,cd->tsd', spread, point_weight[layer], preferred_element_...  52 us
    all_to_all x1, waiting for transfers between devices, local(): lax.all_to_all(outgoing, 'date', split_axis=2, concat_axis=1, tiled=True)  24.9 us
    all_to_all x2, local copies, waits for them, and re-layouts, local(): lax.all_to_all(outgoing, 'date', split_axis=2, concat_axis=1, tiled=True)  23.9 us
    reshape x2, local copies, waits for them, and re-layouts, local(): outgoing = picked.T.reshape(bands, date_dev, table.shape[0])  16.8 us
  transfers between devices with their start and end apart: 3, of which 2 were waited for; matrix products, arithmetic and copies ran while one was open for 37% of the time, Pallas kernels for 0%

profile of v1, /device:TPU:4, one launch (start us, length us, event | category | flops | bytes accessed | tf_op | source)
XLA Modules:
  0.0 677.6 jit_solution(17209050162481803014)
XLA Ops:
  7.3 4.6 reduce-window.14
  13.7 15.6 %scatter_custom_fusion = s32[16384]{0:T(1024)S(1)} fusion(s32[4096]{0:T(1024)S(1)} %bitcast.205, s32[4096]{0:T(1024)S(1)} %iota.39, s32[]{:T(128)} %copy.82), kind=kCustom, calls=%fused_computation.118 | custom fusion | bytes 65540 | tf_op jit(solution)/shard_map/scatter | solution.py:67
  30.1 1.1 reshape.262
  31.8 57.4 %gather_fusion = bf16[16384,40]{1,0:T(8,128)(2,1)} fusion(bf16[4096,40]{1,0:T(8,128)(2,1)S(1)} %bitcast.185, s32[16384]{0:T(1024)S(1)} %broadcast_clamp_fusion), kind=kCustom, calls=%fused_computation | custom fusion | bytes 2686976 | tf_op jit(solution)/shard_map/jit(_take)/gather | solution.py:76
  89.2 13.9 %select_bitcast_fusion = bf16[40,16384]{0,1:T(8,128)(2,1)} fusion(bf16[16384,40]{1,0:T(8,128)(2,1)} %gather_fusion, pred[16384]{0:T(1024)(128)(4,1)S(1)} %compare_and_fusion, pred[16384]{0:T(1024)(128)(4,1)S(1)} %lt.84), kind=kLoop, calls=%fused_computation.60 | loop fusion | flops 1310720 | bytes 2654208 | tf_op jit(solution)/shard_map/jit(_where)/select_n | solution.py:77
  103.1 3.5 copy.48
  107.1 16.3 %copy.49 = bf16[10,4,16384]{0,1,2:T(4,128)(2,1)} copy(bf16[10,4,16384]{2,1,0:T(4,128)(2,1)S(1)} %reshape.264) | data formatting | bytes 2621440 | tf_op jit(solution)/shard_map/reshape | solution.py:78
  123.4 27.2 %reshape.312 = bf16[16,2,20480]{2,1,0:T(2,128)(2,1)} reshape(bf16[16384,4,10]{2,1,0:T(4,128)(2,1)} %bitcast.186) | data formatting | bytes 2621440
  150.6 8.6 %all-to-all-start = ((bf16[16,2,20480]{2,1,0:T(2,128)(2,1)}), bf16[16,2,20480]{2,1,0:T(2,128)(2,1)S(1)}, u32[]{:S(2)}, u32[]{:S(2)}) async-start(bf16[16,2,20480]{2,1,0:T(2,128)(2,1)} %reshape.312), calls=%async_computation | async-start | bytes 2621440 | tf_op jit(solution)/shard_map/all_to_all | solution.py:83
  159.6 1.4 compare_reduce_fusion
  161.0 4.6 reduce-window.16
  166.4 24.9 %all-to-all-done = bf16[16,2,20480]{2,1,0:T(2,128)(2,1)S(1)} async-done(((bf16[16,2,20480]{2,1,0:T(2,128)(2,1)}), bf16[16,2,20480]{2,1,0:T(2,128)(2,1)S(1)}, u32[]{:S(2)}, u32[]{:S(2)}) %all-to-all-start) | async-done | bytes 1310752 | tf_op jit(solution)/shard_map/all_to_all | solution.py:83
  191.4 40.8 %reshape.313 = bf16[16384,4,10]{2,1,0:T(4,128)(2,1)} reshape(bf16[16,2,20480]{2,1,0:T(2,128)(2,1)S(1)} %all-to-all-done) | data formatting | bytes 2621440
  232.2 23.6 %copy.50 = bf16[10,4,16,1024]{3,1,2,0:T(4,128)(2,1)S(1)} copy(bf16[10,4,16,1024]{0,1,3,2:T(4,128)(2,1)} %bitcast.187) | data formatting | bytes 2621440 | tf_op jit(solution)/shard_map/all_to_all | solution.py:83
  268.0 5.2 reshape.314
  273.2 7.5 %all-to-all-start.1 = ((bf16[16,2,20480]{2,1,0:T(2,128)(2,1)}), bf16[16,2,20480]{2,1,0:T(2,128)(2,1)}, u32[]{:S(2)}, u32[]{:S(2)}) async-start(bf16[16,2,20480]{2,1,0:T(2,128)(2,1)} %reshape.314), calls=%async_computation.1 | async-start | bytes 2621440 | tf_op jit(solution)/shard_map/all_to_all | solution.py:80
  281.4 240.3 %scatter_custom_fusion.1 = s32[16385]{0:T(1024)S(1)} fusion(s32[65536]{0:T(1024)S(1)} %bitcast.197, s32[65536]{0:T(1024)} %param.14, s32[]{:T(128)} %constant.109.clone.1), kind=kCustom, calls=%fused_computation.115 | custom fusion | bytes 66052 | tf_op jit(solution)/shard_map/scatter | solution.py:99
  522.7 4.3 reshape.315
  526.9 3.5 copy.51
  530.5 4.2 reshape_reshape.4
  535.5 77.0 %while.13 = (s32[]{:T(128)}, f32[2,16,16,128]{3,2,1,0:T(8,128)}, f32[2,5,128]{2,1,0:T(8,128)S(1)}, bf16[2,10,64,512]{3,1,2,0:T(8,128)(2,1)S(1)}, bf16[10,128]{1,...) while((s32[]{:T(128)}, f32[2,16,16,128]{3,2,1,0:T(8,128)}, ...), condition=%wide.region_9.10_spmd.clone, body=%wide.region_8.9_spmd.clone.sunk | while | flops 1861231104 | bytes 78875824 | solution.py:115
  535.9 4.7 convolution_convert_fusion.2
  540.6 21.0 %add_maximum_fusion.4 = f32[64,512,128]{2,1,0:T(8,128)} fusion(f32[128]{0:T(128)S(1)} %get-tuple-element.364, f32[128]{0:T(128)S(1)} %get-tuple-element.365, f32[128]{0:T(128)S(1)} %get-tuple-element.366, bf16[64,512,128]{2,1,0:T(8,128)(2,1)} %convolution_convert_fusion.2, f32[128]{0:T(128)S(1)} %get-tuple-element.367, ...), kind=kOutput, calls=%fused_computation.5.clone.1 | convolution fusion | flops 1153433600 | bytes 25202688 | tf_op jit(solution)/shard_map/while/body/eval_jaxpr/tsc,cd->tsd/dot_general | solution.py:24
  561.6 6.4 multiply_convert_fusion.10
  568.0 4.9 add_maximum_fusion.5
  574.2 4.7 convolution_convert_fusion.2
  578.9 21.0 %add_maximum_fusion.4 = f32[64,512,128]{2,1,0:T(8,128)} fusion(f32[128]{0:T(128)S(1)} %get-tuple-element.364, f32[128]{0:T(128)S(1)} %get-tuple-element.365, f32[128]{0:T(128)S(1)} %get-tuple-element.366, bf16[64,512,128]{2,1,0:T(8,128)(2,1)} %convolution_convert_fusion.2, f32[128]{0:T(128)S(1)} %get-tuple-element.367, ...), kind=kOutput, calls=%fused_computation.5.clone.1 | convolution fusion | flops 1153433600 | bytes 25202688 | tf_op jit(solution)/shard_map/while/body/eval_jaxpr/tsc,cd->tsd/dot_general | solution.py:24
  600.0 6.4 multiply_convert_fusion.10
  606.4 4.9 add_maximum_fusion.5
  612.6 1.6 reduce_sum.38
  615.0 54.4 %reduce-scatter.2.cloned.1.call-done = f32[1,16,128]{2,1,0:T(8,128)} async-done(((f32[16,16,128]{2,1,0:T(8,128)}), f32[1,16,128]{2,1,0:T(8,128)}) %reduce-scatter.2.cloned.1.call-update) | async-done | bytes 8208 | tf_op jit(solution)/shard_map/reduce_scatter | solution.py:116
  669.4 1.4 broadcast_divide_fusion
  (104 shorter events, 23.5 us)
Async XLA Ops:
  123.4 36.2 %copy-start = (s32[65536,1]{0,1:T(1,128)S(1)}, s32[65536,1]{0,1:T(1,128)}, u32[]{:S(2)}) copy-start(s32[65536,1]{0,1:T(1,128)} %param.13) | copy-start | bytes 786436
  150.6 40.8 %all-to-all-start = ((bf16[16,2,20480]{2,1,0:T(2,128)(2,1)}), bf16[16,2,20480]{2,1,0:T(2,128)(2,1)S(1)}, u32[]{:S(2)}, u32[]{:S(2)}) async-start(bf16[16,2,20480]{2,1,0:T(2,128)(2,1)} %reshape.312), calls=%async_computation | async-start | bytes 2621440 | tf_op jit(solution)/shard_map/all_to_all | solution.py:83
  266.5 14.9 %copy-start.10 = (f32[2,5,128]{2,0,1:T(2,128)S(1)}, f32[2,5,128]{2,0,1:T(2,128)}, u32[]{:S(2)}) copy-start(f32[2,5,128]{2,0,1:T(2,128)} %param.16) | copy-start | bytes 15364
  273.2 249.5 %all-to-all-start.1 = ((bf16[16,2,20480]{2,1,0:T(2,128)(2,1)}), bf16[16,2,20480]{2,1,0:T(2,128)(2,1)}, u32[]{:S(2)}, u32[]{:S(2)}) async-start(bf16[16,2,20480]{2,1,0:T(2,128)(2,1)} %reshape.314), calls=%async_computation.1 | async-start | bytes 2621440 | tf_op jit(solution)/shard_map/all_to_all | solution.py:80
  280.6 388.8 %reduce-scatter.2.cloned.1.call-start = ((), (), s32[]{:S(2)}) async-start(), calls=%async_computation.3 | async-start | bytes 139264 | tf_op jit(solution)/shard_map/reduce_scatter | solution.py:116
  530.4 5.0 copy-start.5
  530.4 5.1 copy-start.6
  530.4 5.1 copy-start.7
  530.4 5.1 copy-start.8
  530.4 5.1 copy-start.9
  530.4 5.1 copy-start.11
  535.5 78.7 %copy-start.1 = (s32[65536]{0:T(1024)S(1)}, s32[65536]{0:T(1024)}, u32[]{:S(2)}) copy-start(s32[65536]{0:T(1024)} %param.14) | copy-start | bytes 786436
  535.5 78.7 %copy-start.4 = (pred[65536]{0:T(1024)(128)(4,1)S(1)}, pred[65536]{0:T(1024)(128)(4,1)}, u32[]{:S(2)}) copy-start(pred[65536]{0:T(1024)(128)(4,1)} %get-tuple-element.276) | copy-start | bytes 196612
  568.0 5.0 copy-start.2
  573.5 0.7 copy-start.3
  606.4 5.0 copy-start.2
  611.9 0.7 copy-start.3
Sparse Core Ops, SparseCore 0:
  614.3 55.0 reduce-scatter.1
